TPU v7x, 32 devices: a whole 2x2x4 slice. The times are simulated.
32 devices in a mesh: grp: 2 (over y), rows: 8 (over z, x), mod: 2 (over core).
Axes of the slice: x: 2, y: 2, z: 4, core: 2. Of those that a mesh axis runs over, the one named last changes fastest.
Arguments:
- queries: bfloat16 [16, 8, 2304], P(('grp', 'rows'), 'mod'), parts along dimension 0, may hold values from -6 to 6
- train_grads: bfloat16 [2048, 8, 2304], P(('grp', 'rows'), 'mod'), parts along dimension 0, may hold values from -6 to 6
- factors: float32 [8, 2, 48, 48], P('mod'), may hold values from -4 to 4, as said below
Outputs:
- scores: float32 [16, 1024], P(('grp', 'mod'), 'rows'), parts along dimension 0
There are 2 independent parts, one for each index of `grp`. A program takes and returns all parts, laid end to end along the dimension named above; an argument that names none is the same for every part. Nothing has to cross between parts.
Inputs may be any that keep to these rules, and one draw needn't show every extreme that they name: `factors`: each factor is a 48 x 48 matrix with a positive diagonal and full rank.
All inputs are finite; a program needn't handle non-finite values.
Results may differ from a plain program's by a relative error of at most 0.0029.
Values may be sent and summed in bfloat16 or wider, within the bound.
No kernel may reach another device: no remote copies, remote signals or barrier semaphores. Data moves between devices by JAX's collectives and lax.ppermute only.
A program may use at most 64 MiB of HBM per device.

v0:
```python
import jax
import jax.numpy as jnp
from jax import lax
from jax.sharding import PartitionSpec as P

MODULES = 8
PROJ = 48
COORDS = 2304


def precondition(grads_in, factors):
    count = grads_in.shape[0]
    local_modules = grads_in.shape[1]
    grads = grads_in.astype(jnp.float32).reshape(count, local_modules, PROJ, PROJ)
    left_side = jnp.einsum("mab,qmbc->qmac", factors[:, 0], grads, precision=lax.Precision.HIGHEST)
    both_sides = jnp.einsum(
        "qmac,mcd->qmad", left_side, factors[:, 1], precision=lax.Precision.HIGHEST
    )
    both_sides = both_sides / jnp.sqrt(jnp.float32(MODULES * COORDS))
    return both_sides.astype(jnp.bfloat16).reshape(count, local_modules, PROJ * PROJ)


def shards(queries, train_grads, factors):
    train_count = train_grads.shape[0]
    train_flat = train_grads.reshape(train_count, -1)
    scaled_own = precondition(queries, factors)
    ready_rows = lax.all_gather(scaled_own, "rows", axis=0, tiled=True)
    flat_rows = ready_rows.reshape(ready_rows.shape[0], -1)
    partial_value = lax.dot_general(
        flat_rows, train_flat, (((1,), (1,)), ((), ())), preferred_element_type=jnp.float32
    )
    return lax.psum_scatter(partial_value, "mod", scatter_dimension=0, tiled=True)


def solution(mesh):
    in_specs = (
        P(("grp", "rows"), "mod", None),
        P(("grp", "rows"), "mod", None),
        P("mod", None, None, None),
    )
    out_specs = P(("grp", "mod"), "rows")
    return jax.shard_map(shards, mesh=mesh, in_specs=in_specs, out_specs=out_specs, check_vma=False)
```

profile of v0, /device:TPU:0, one launch (start us, length us, event | category | flops | bytes accessed | tf_op | source)
XLA Modules:
  0.0 40.9 jit_solution(16463728505834022918)
XLA Ops:
  0.0 0.0 copy-start
  0.0 0.0 copy-start.1
  0.0 1.0 %reshape.18 = bf16[4,48,48]{2,1,0:T(8,128)(2,1)S(1)} reshape(bf16[1,4,2304]{2,1,0:T(4,128)(2,1)} %param.3) | data formatting | bytes 36864 | tf_op jit(solution)/shard_map/reshape
  1.0 1.2 %convolution_bitcast_fusion = f32[4,48,48]{1,2,0:T(8,128)S(1)} fusion(bf16[4,48,48]{2,1,0:T(8,128)(2,1)S(1)} %reshape.18, f32[4,2,48,48]{3,2,1,0:T(8,128)} %param.5), kind=kOutput, calls=%fused_computation.3 | convolution fusion | flops 5308416 | bytes 153600 | tf_op jit(solution)/shard_map/mab,qmbc->qmac/dot_general | solution.py:15
  2.1 1.2 %fusion.3 = bf16[1,4,48,48]{3,2,1,0:T(8,128)(2,1)S(1)} fusion(f32[4,48,48]{1,2,0:T(8,128)S(1)} %convolution_bitcast_fusion, f32[4,2,48,48]{3,2,1,0:T(8,128)} %param.5), kind=kOutput, calls=%fused_computation.5 | convolution fusion | flops 5326848 | bytes 153600 | tf_op jit(solution)/shard_map/qmac,mcd->qmad/dot_general | solution.py:16
  3.4 0.1 reshape.20
  3.5 32.4 %all_gather.3 = bf16[8,4,2304]{2,1,0:T(4,128)(2,1)S(1)} all-gather(bf16[1,4,2304]{2,1,0:T(4,128)(2,1)S(1)} %reshape.20), channel_id=1, replica_groups=mesh['grp'=2,'rows'=8,'mod'=2] {'rows'}, dimensions={0}, use_global_device_ids=true | all-gather | bytes 165888 | tf_op jit(solution)/shard_map/all_gather | solution.py:27
  35.9 0.0 copy-done
  35.9 0.7 %fusion.4 = f32[8,128]{1,0:T(8,128)S(1)} fusion(bf16[128,4,2304]{2,1,0:T(4,128)(2,1)S(1)} %copy-done, bf16[8,4,2304]{2,1,0:T(4,128)(2,1)S(1)} %all_gather.3), kind=kOutput, calls=%fused_computation.6 | convolution fusion | flops 18874368 | bytes 2510848 | tf_op jit(solution)/shard_map/dot_general | solution.py:29
  36.6 2.5 %all-reduce = f32[8,128]{1,0:T(8,128)S(1)} all-reduce(f32[8,128]{1,0:T(8,128)S(1)} %fusion.4), channel_id=2, replica_groups=mesh['grp'=2,'rows'=8,'mod'=2] {'mod'}, use_global_device_ids=true, to_apply=%region_0.0.clone | all-reduce | flops 1024 | bytes 8192
  39.1 0.0 copy-done.1
  39.1 0.6 %dynamic-slice = u32[1]{0:T(128)} dynamic-slice(u32[32]{0:T(128)S(1)} %copy-done.1, u32[]{:T(128)S(6)} %add.3), dynamic_slice_sizes={1} | dynamic-slice | bytes 12
  40.3 0.6 %constant_dynamic-slice_fusion = f32[4,128]{1,0:T(4,128)} fusion(f32[8,128]{1,0:T(8,128)S(1)} %all-reduce, u32[]{:T(128)S(6)} %multiply.5), kind=kLoop, calls=%fused_computation.12 | loop fusion | bytes 4100
Async XLA Ops:
  0.0 35.9 %copy-start = (bf16[128,4,2304]{2,1,0:T(4,128)(2,1)S(1)}, bf16[128,4,2304]{2,1,0:T(4,128)(2,1)}, u32[]{:S(2)}) copy-start(bf16[128,4,2304]{2,1,0:T(4,128)(2,1)} %param.4) | copy-start | bytes 7077892
  0.0 39.1 %copy-start.1 = (u32[32]{0:T(128)S(1)}, u32[32]{0:T(128)}, u32[]{:S(2)}) copy-start(u32[32]{0:T(128)} %constant.6) | copy-start | bytes 388
where the time goes:
time: 41.1 us; the launch traced here: 40.9 us
  blocking collectives  34.8 us (85%)
  matrix products  3.1 us (8%)
  local copies, waits for them, and re-layouts  2.27 us (6%)
  between operations  0.68 us (2%)
    all_gather x1, blocking collectives, shards(): ready_rows = lax.all_gather(scaled_own, 'rows', axis=0, tiled=True)  32.4 us
    unnamed x1, blocking collectives  2.46 us
    dot_general x1, matrix products, precondition(): jnp.einsum('qmac,mcd->qmad', left_side, factors[:, 1], precision=lax.Prec...  1.24 us
    unnamed x6, local copies, waits for them, and re-layouts  1.18 us
    dot_general x1, matrix products, precondition(): jnp.einsum('mab,qmbc->qmac', factors[:, 0], grads, precision=lax.Precisio...  1.15 us
    reshape x1, local copies, waits for them, and re-layouts  0.98 us

commit v1 on v0

--- a/solution.py
+++ b/solution.py
@@ -6,6 +6,12 @@
 MODULES = 8
 PROJ = 48
 COORDS = 2304
+
+
+def in_order(parts, dim):
+    parts = jnp.moveaxis(parts, 0, dim)
+    lengths = parts.shape
+    return parts.reshape(*lengths[:dim], lengths[dim] * lengths[dim + 1], *lengths[dim + 2 :])
 
 
 def precondition(grads_in, factors):
@@ -24,7 +30,19 @@
     train_count = train_grads.shape[0]
     train_flat = train_grads.reshape(train_count, -1)
     scaled_own = precondition(queries, factors)
-    ready_rows = lax.all_gather(scaled_own, "rows", axis=0, tiled=True)
+    peers = lax.axis_size("rows")
+    pairs = [(i, (i + 1) % peers) for i in range(peers)]
+    back = [(b, a) for a, b in pairs]
+    lower, upper = ([], [])
+    for step in range(peers - 1):
+        if step % 2 == 0:
+            lower.append(lax.ppermute(lower[-1] if lower else scaled_own, "rows", pairs))
+        else:
+            upper.append(lax.ppermute(upper[-1] if upper else scaled_own, "rows", back))
+    blocks = jnp.stack([*lower[::-1], scaled_own, *upper])
+    shift = lax.axis_index("rows") - len(lower)
+    blocks = blocks[(jnp.arange(peers) - shift) % peers]
+    ready_rows = in_order(blocks, 0)
     flat_rows = ready_rows.reshape(ready_rows.shape[0], -1)
     partial_value = lax.dot_general(
         flat_rows, train_flat, (((1,), (1,)), ((), ())), preferred_element_type=jnp.float32

time: 41.1 us -> 38.5 us (0.937)
  blocking collectives: 34.8 us -> 2.47 us
  starting transfers between devices: 0 us -> 17.3 us
  waiting for transfers between devices: 0 us -> 9.5 us
  local copies, waits for them, and re-layouts: 2.27 us -> 5.02 us
    all_gather x1 -> x0, blocking collectives: 32.4 us -> none  [shards(): ready_rows = lax.all_gather(scaled_own, 'rows', axis=0, tiled=True)]
    ppermute x0 -> x7, starting transfers between devices: none -> 17.3 us  [the longest x3 14.3 us: shards(): upper.append(lax.ppermute(upper[-1] if upper else scaled_own, 'rows', back))]
    ppermute x0 -> x7, waiting for transfers between devices: none -> 9.5 us  [the longest x4 8.18 us: shards(): lax.ppermute(lower[-1] if lower else scaled_own, 'rows', pairs)]
    unnamed x6 -> x13, local copies, waits for them, and re-layouts: 1.18 us -> 3.27 us
    gather x0 -> x1, local copies, waits for them, and re-layouts: none -> 0.67 us  [shards(): blocks = blocks[(jnp.arange(peers) - shift) % peers]]
  transfers between devices with their start and end apart: 0 -> 7, of which waited for: 0 -> 4; matrix products, arithmetic and copies ran while one was open for 0% -> 7% of each run, Pallas kernels for 0% -> 0%
where the time goes in v1:
time: 38.5 us; the launch traced here: 38.2 us
  starting transfers between devices  17.3 us (45%)
  waiting for transfers between devices  9.5 us (25%)
  local copies, waits for them, and re-layouts  5.02 us (13%)
  matrix products  3.09 us (8%)
  blocking collectives  2.47 us (6%)
  between operations  0.8 us (2%)
    ppermute x3, starting transfers between devices, shards(): upper.append(lax.ppermute(upper[-1] if upper else scaled_own, 'rows', back))  14.3 us
    ppermute x4, waiting for transfers between devices, shards(): lax.ppermute(lower[-1] if lower else scaled_own, 'rows', pairs)  8.18 us
    unnamed x13, local copies, waits for them, and re-layouts  3.27 us
    ppermute x4, starting transfers between devices, shards(): lax.ppermute(lower[-1] if lower else scaled_own, 'rows', pairs)  3.03 us
    unnamed x1, blocking collectives  2.47 us
    ppermute x3, waiting for transfers between devices, shards(): upper.append(lax.ppermute(upper[-1] if upper else scaled_own, 'rows', back))  1.32 us
    dot_general x1, matrix products, precondition(): jnp.einsum('qmac,mcd->qmad', left_side, factors[:, 1], precision=lax.Prec...  1.24 us
    dot_general x1, matrix products, precondition(): jnp.einsum('mab,qmbc->qmac', factors[:, 0], grads, precision=lax.Precisio...  1.15 us
  transfers between devices with their start and end apart: 7, of which 4 were waited for; matrix products, arithmetic and copies ran while one was open for 7% of the time, Pallas kernels for 0%

profile of v1, /device:TPU:0, one launch (start us, length us, event | category | flops | bytes accessed | tf_op | source)
XLA Modules:
  0.0 38.2 jit_solution(17174488440000834090)
XLA Ops:
  0.0 0.8 %reshape.68 = bf16[4,48,48]{2,1,0:T(8,128)(2,1)S(1)} reshape(bf16[1,4,2304]{2,1,0:T(4,128)(2,1)} %param.3) | data formatting | bytes 36864 | tf_op jit(solution)/shard_map/reshape
  0.8 1.2 %convolution_bitcast_fusion = f32[4,48,48]{1,2,0:T(8,128)S(1)} fusion(bf16[4,48,48]{2,1,0:T(8,128)(2,1)S(1)} %reshape.68, f32[4,2,48,48]{3,2,1,0:T(8,128)} %param.5), kind=kOutput, calls=%fused_computation.2 | convolution fusion | flops 5308416 | bytes 153600 | tf_op jit(solution)/shard_map/mab,qmbc->qmac/dot_general | solution.py:21
  2.0 1.2 %fusion.1 = bf16[1,4,48,48]{3,2,1,0:T(8,128)(2,1)S(1)} fusion(f32[4,48,48]{1,2,0:T(8,128)S(1)} %convolution_bitcast_fusion, f32[4,2,48,48]{3,2,1,0:T(8,128)} %param.5), kind=kOutput, calls=%fused_computation.4 | convolution fusion | flops 5326848 | bytes 153600 | tf_op jit(solution)/shard_map/qmac,mcd->qmad/dot_general | solution.py:22
  3.2 0.1 reshape.70
  3.4 3.0 %collective-permute-start = (bf16[1,4,2304]{2,1,0:T(4,128)(2,1)S(1)}, bf16[1,4,2304]{2,1,0:T(4,128)(2,1)S(1)}, u32[]{:S(2)}, u32[]{:S(2)}) collective-permute-start(bf16[1,4,2304]{2,1,0:T(4,128)(2,1)S(1)} %reshape.70), channel_id=1, source_target_pairs={{0,2},{2,4},{4,6},{6,8},{8,10},{10,12},{12,14},{14,0},{1,3},{3,5},... | collective-permute-start | bytes 55304 | tf_op jit(solution)/shard_map/ppermute | solution.py:39
  6.4 4.8 %collective-permute-done = bf16[1,4,2304]{2,1,0:T(4,128)(2,1)S(1)} collective-permute-done((bf16[1,4,2304]{2,1,0:T(4,128)(2,1)S(1)}, bf16[1,4,2304]{2,1,0:T(4,128)(2,1)S(1)}, u32[]{:S(2)}, u32[]{:S(2)}) %collective-permute-start) | collective-permute-done | bytes 18464 | tf_op jit(solution)/shard_map/ppermute | solution.py:39
  11.2 0.0 collective-permute-start.1
  11.2 4.7 %collective-permute-start.4 = (bf16[1,4,2304]{2,1,0:T(4,128)(2,1)S(1)}, bf16[1,4,2304]{2,1,0:T(4,128)(2,1)S(1)}, u32[]{:S(2)}, u32[]{:S(2)}) collective-permute-start(bf16[1,4,2304]{2,1,0:T(4,128)(2,1)S(1)} %reshape.70), channel_id=1, source_target_pairs={{2,0},{4,2},{6,4},{8,6},{10,8},{12,10},{14,12},{0,14},{3,1},{5,3},... | collective-permute-start | bytes 55304 | tf_op jit(solution)/shard_map/ppermute | solution.py:41
  15.9 1.7 %collective-permute-done.1 = bf16[1,4,2304]{2,1,0:T(4,128)(2,1)S(1)} collective-permute-done((bf16[1,4,2304]{2,1,0:T(4,128)(2,1)S(1)}, bf16[1,4,2304]{2,1,0:T(4,128)(2,1)S(1)}, u32[]{:S(2)}, u32[]{:S(2)}) %collective-permute-start.1) | collective-permute-done | bytes 18464 | tf_op jit(solution)/shard_map/ppermute | solution.py:39
  17.6 0.0 collective-permute-start.2
  17.6 0.0 collective-permute-done.4
  17.6 4.8 %collective-permute-start.5 = (bf16[1,4,2304]{2,1,0:T(4,128)(2,1)S(1)}, bf16[1,4,2304]{2,1,0:T(4,128)(2,1)S(1)}, u32[]{:S(2)}, u32[]{:S(2)}) collective-permute-start(bf16[1,4,2304]{2,1,0:T(4,128)(2,1)S(1)} %collective-permute-done.4), channel_id=1, source_target_pairs={{2,0},{4,2},{6,4},{8,6},{10,8},{12,10},{14,12},{0,14},{3,1},{5,3},... | collective-permute-start | bytes 55304 | tf_op jit(solution)/shard_map/ppermute | solution.py:41
  22.4 1.7 %collective-permute-done.2 = bf16[1,4,2304]{2,1,0:T(4,128)(2,1)S(1)} collective-permute-done((bf16[1,4,2304]{2,1,0:T(4,128)(2,1)S(1)}, bf16[1,4,2304]{2,1,0:T(4,128)(2,1)S(1)}, u32[]{:S(2)}, u32[]{:S(2)}) %collective-permute-start.2) | collective-permute-done | bytes 18464 | tf_op jit(solution)/shard_map/ppermute | solution.py:39
  24.1 0.1 stack_reshape.3
  24.2 0.0 copy-start
  24.2 2.0 %copy.17 = bf16[16,8,4,2304]{3,1,2,0:T(8,128)(2,1)S(1)} copy(bf16[16,8,4,2304]{3,2,1,0:T(4,128)(2,1)} %bitcast.53) | data formatting | bytes 4718592
  26.2 0.6 %dynamic-slice = u32[1]{0:T(128)} dynamic-slice(u32[32]{0:T(128)S(1)} %copy-done, u32[]{:T(128)S(6)} %add.29), dynamic_slice_sizes={1} | dynamic-slice | bytes 12
  27.5 4.8 %collective-permute-start.6 = (bf16[1,4,2304]{2,1,0:T(4,128)(2,1)S(1)}, bf16[1,4,2304]{2,1,0:T(4,128)(2,1)S(1)}, u32[]{:S(2)}, u32[]{:S(2)}) collective-permute-start(bf16[1,4,2304]{2,1,0:T(4,128)(2,1)S(1)} %collective-permute-done.5), channel_id=1, source_target_pairs={{2,0},{4,2},{6,4},{8,6},{10,8},{12,10},{14,12},{0,14},{3,1},{5,3},... | collective-permute-start | bytes 55304 | tf_op jit(solution)/shard_map/ppermute | solution.py:41
  32.2 0.0 collective-permute-done.3
  32.4 1.3 %collective-permute-done.6 = bf16[1,4,2304]{2,1,0:T(4,128)(2,1)S(1)} collective-permute-done((bf16[1,4,2304]{2,1,0:T(4,128)(2,1)S(1)}, bf16[1,4,2304]{2,1,0:T(4,128)(2,1)S(1)}, u32[]{:S(2)}, u32[]{:S(2)}) %collective-permute-start.6) | collective-permute-done | bytes 18464 | tf_op jit(solution)/shard_map/ppermute | solution.py:41
  33.7 0.7 %gather_fusion = bf16[8,4,2304]{2,1,0:T(4,128)(2,1)S(1)} fusion(bf16[8,4,2304]{2,1,0:T(4,128)(2,1)S(1)} %bitcast.56, s32[1024]{0:T(1024)S(1)} %pad_clamp_fusion), kind=kCustom, calls=%fused_computation | custom fusion | bytes 294944 | tf_op jit(solution)/shard_map/gather | solution.py:44
  34.4 0.7 %fusion.8 = f32[8,128]{1,0:T(8,128)S(1)} fusion(bf16[8,9216]{1,0:T(8,128)(2,1)S(1)} %bitcast.54, bf16[128,9216]{1,0:T(8,128)(2,1)S(1)} %bitcast.52), kind=kOutput, calls=%fused_computation.25 | convolution fusion | flops 18874368 | bytes 2510848 | tf_op jit(solution)/shard_map/dot_general | solution.py:47
  35.1 2.5 %all-reduce = f32[8,128]{1,0:T(8,128)S(1)} all-reduce(f32[8,128]{1,0:T(8,128)S(1)} %fusion.8), channel_id=2, replica_groups=mesh['grp'=2,'rows'=8,'mod'=2] {'mod'}, use_global_device_ids=true, to_apply=%region_0.1.clone | all-reduce | flops 1024 | bytes 8192
  37.6 0.6 %constant_dynamic-slice_fusion = f32[4,128]{1,0:T(4,128)} fusion(f32[8,128]{1,0:T(8,128)S(1)} %all-reduce, u32[]{:T(128)S(6)} %multiply.5), kind=kLoop, calls=%fused_computation.24 | loop fusion | bytes 4100
  (14 shorter events, 0.2 us)
Async XLA Ops:
  3.4 7.8 %collective-permute-start = (bf16[1,4,2304]{2,1,0:T(4,128)(2,1)S(1)}, bf16[1,4,2304]{2,1,0:T(4,128)(2,1)S(1)}, u32[]{:S(2)}, u32[]{:S(2)}) collective-permute-start(bf16[1,4,2304]{2,1,0:T(4,128)(2,1)S(1)} %reshape.70), channel_id=1, source_target_pairs={{0,2},{2,4},{4,6},{6,8},{8,10},{10,12},{12,14},{14,0},{1,3},{3,5},... | collective-permute-start | bytes 55304 | tf_op jit(solution)/shard_map/ppermute | solution.py:39
  11.2 6.5 %collective-permute-start.1 = (bf16[1,4,2304]{2,1,0:T(4,128)(2,1)S(1)}, bf16[1,4,2304]{2,1,0:T(4,128)(2,1)S(1)}, u32[]{:S(2)}, u32[]{:S(2)}) collective-permute-start(bf16[1,4,2304]{2,1,0:T(4,128)(2,1)S(1)} %collective-permute-done), channel_id=1, source_target_pairs={{0,2},{2,4},{4,6},{6,8},{8,10},{10,12},{12,14},{14,0},{1,3},{3,5},... | collective-permute-start | bytes 55304 | tf_op jit(solution)/shard_map/ppermute | solution.py:39
  11.2 6.5 %collective-permute-start.4 = (bf16[1,4,2304]{2,1,0:T(4,128)(2,1)S(1)}, bf16[1,4,2304]{2,1,0:T(4,128)(2,1)S(1)}, u32[]{:S(2)}, u32[]{:S(2)}) collective-permute-start(bf16[1,4,2304]{2,1,0:T(4,128)(2,1)S(1)} %reshape.70), channel_id=1, source_target_pairs={{2,0},{4,2},{6,4},{8,6},{10,8},{12,10},{14,12},{0,14},{3,1},{5,3},... | collective-permute-start | bytes 55304 | tf_op jit(solution)/shard_map/ppermute | solution.py:41
  17.6 6.5 %collective-permute-start.2 = (bf16[1,4,2304]{2,1,0:T(4,128)(2,1)S(1)}, bf16[1,4,2304]{2,1,0:T(4,128)(2,1)S(1)}, u32[]{:S(2)}, u32[]{:S(2)}) collective-permute-start(bf16[1,4,2304]{2,1,0:T(4,128)(2,1)S(1)} %collective-permute-done.1), channel_id=1, source_target_pairs={{0,2},{2,4},{4,6},{6,8},{8,10},{10,12},{12,14},{14,0},{1,3},{3,5},... | collective-permute-start | bytes 55304 | tf_op jit(solution)/shard_map/ppermute | solution.py:39
  17.6 9.8 %collective-permute-start.5 = (bf16[1,4,2304]{2,1,0:T(4,128)(2,1)S(1)}, bf16[1,4,2304]{2,1,0:T(4,128)(2,1)S(1)}, u32[]{:S(2)}, u32[]{:S(2)}) collective-permute-start(bf16[1,4,2304]{2,1,0:T(4,128)(2,1)S(1)} %collective-permute-done.4), channel_id=1, source_target_pairs={{2,0},{4,2},{6,4},{8,6},{10,8},{12,10},{14,12},{0,14},{3,1},{5,3},... | collective-permute-start | bytes 55304 | tf_op jit(solution)/shard_map/ppermute | solution.py:41
  24.1 8.2 %collective-permute-start.3 = (bf16[1,4,2304]{2,1,0:T(4,128)(2,1)S(1)}, bf16[1,4,2304]{2,1,0:T(4,128)(2,1)S(1)}, u32[]{:S(2)}, u32[]{:S(2)}) collective-permute-start(bf16[1,4,2304]{2,1,0:T(4,128)(2,1)S(1)} %collective-permute-done.2), channel_id=1, source_target_pairs={{0,2},{2,4},{4,6},{6,8},{8,10},{10,12},{12,14},{14,0},{1,3},{3,5},... | collective-permute-start | bytes 55304 | tf_op jit(solution)/shard_map/ppermute | solution.py:39
  24.2 2.0 %copy-start = (u32[32]{0:T(128)S(1)}, u32[32]{0:T(128)}, u32[]{:S(2)}) copy-start(u32[32]{0:T(128)} %constant.32) | copy-start | bytes 388
  27.5 6.2 %collective-permute-start.6 = (bf16[1,4,2304]{2,1,0:T(4,128)(2,1)S(1)}, bf16[1,4,2304]{2,1,0:T(4,128)(2,1)S(1)}, u32[]{:S(2)}, u32[]{:S(2)}) collective-permute-start(bf16[1,4,2304]{2,1,0:T(4,128)(2,1)S(1)} %collective-permute-done.5), channel_id=1, source_target_pairs={{2,0},{4,2},{6,4},{8,6},{10,8},{12,10},{14,12},{0,14},{3,1},{5,3},... | collective-permute-start | bytes 55304 | tf_op jit(solution)/shard_map/ppermute | solution.py:41
